TPU v7x, 512 devices: a whole 4x4x16 slice. The times are simulated.
512 devices in a mesh: section: 8 (over y_hi, x), head: 4 (over y_lo, core), tok: 16 (over z).
Axes of the slice: x: 4, y: 4 (y_hi: 2, y_lo: 2; y = y_hi * 2 + y_lo), z: 16, core: 2. Of those that a mesh axis runs over, the one named last changes fastest.
Arguments:
- held_cotangents: bfloat16 [8, 2, 2048, 2560], P('section', None, 'tok', 'head'), may hold values from -6 to 6
- entering_adjoint: bfloat16 [2048, 2560], P('tok', 'head'), may hold values from -6 to 6
- saved_queries: bfloat16 [8, 2048, 2560], P('section', 'tok', 'head'), may hold values from -1024 to 1024
- saved_keys: bfloat16 [8, 2048, 2560], P('section', 'tok', 'head'), may hold values from -20 to 20
- value_weight: bfloat16 [8, 2560, 2560], P('section', None, 'head'), may hold values from -0.125 to 0.125
- out_weight: bfloat16 [8, 2560, 2560], P('section', 'tok', 'head'), may hold values from -0.125 to 0.125
- block_gate: float32 [8, 2560], P('section'), may hold values from -3 to 3
- time_gate: float32 [32, 2560], replicated, may hold values from -3 to 3
- timestep: int32 [1], replicated, may hold values from 0 to 31
Outputs:
- passed: bfloat16 [8, 2, 2048, 2560], P('section', None, 'tok', 'head')
All inputs are finite; a program needn't handle non-finite values.
Results may differ from a plain program's by a relative error of at most 0.0085.
Values may be sent and summed in bfloat16 or wider, within the bound.
A program may use at most 64 MiB of HBM per device.

v0:
```python
import jax
import jax.numpy as jnp
from jax import lax
from jax.sharding import PartitionSpec as P

HD = 128
GUIDE = 3.0


def shifted(value, axis, steps):
    count = lax.axis_size(axis)
    leading, last = (max(0, -steps), min(count, count - steps))
    return lax.ppermute(value, axis, [(source, source + steps) for source in range(leading, last)])


def shards(
    held_cotangents,
    entering_adjoint,
    saved_queries,
    saved_keys,
    value_weight,
    out_weight,
    block_gate,
    time_gate,
    timestep,
):
    steps_index = jnp.arange(time_gate.shape[0])
    time_row = jnp.sum(
        jnp.where((steps_index == timestep[0])[:, None], time_gate, jnp.zeros_like(time_gate)),
        axis=0,
    )
    gate_row = block_gate[0] + time_row
    whole_cot = lax.all_gather(held_cotangents[0], "head", axis=2, tiled=True)
    scaled = (whole_cot.astype(jnp.float32) * gate_row).astype(jnp.bfloat16)
    out_full = lax.all_gather(out_weight[0], "tok", axis=0, tiled=True)
    attn_grad = jnp.einsum(
        "btd,dk->btk", scaled, out_full, preferred_element_type=jnp.float32
    ).astype(jnp.bfloat16)
    rows_here = saved_queries.shape[1]
    groups_here = saved_queries.shape[2] // HD
    score_scale = HD ** (-0.5)
    normal_grad = attn_grad[0]
    key_all = lax.all_gather(saved_keys[0], "tok", axis=0, tiled=True)
    key_heads = key_all.reshape(key_all.shape[0], groups_here, HD)
    query_heads = saved_queries[0].reshape(rows_here, groups_here, HD)
    scores = (
        jnp.einsum("ihe,jhe->hij", query_heads, key_heads, preferred_element_type=jnp.float32)
        * score_scale
    )
    row_top = jnp.max(scores, axis=2, keepdims=True)
    log_total = row_top + jnp.log(jnp.sum(jnp.exp(scores - row_top), axis=2, keepdims=True))
    weights = jnp.exp(scores - log_total).astype(jnp.bfloat16)
    grad_heads = normal_grad.reshape(rows_here, groups_here, HD)
    terms = jnp.einsum("hij,ihe->jhe", weights, grad_heads, preferred_element_type=jnp.float32)
    value_grad = lax.psum_scatter(
        terms.reshape(lax.axis_size("tok") * rows_here, groups_here * HD).astype(jnp.bfloat16),
        "tok",
        scatter_dimension=0,
        tiled=True,
    )
    stacked = jnp.stack([value_grad, attn_grad[1]])
    partial_back = jnp.einsum(
        "btk,dk->btd", stacked, value_weight[0], preferred_element_type=jnp.float32
    )
    back_sum = lax.psum_scatter(
        partial_back.astype(jnp.bfloat16), "head", scatter_dimension=2, tiled=True
    ).astype(jnp.float32)
    block_cot = (held_cotangents[0].astype(jnp.float32) + back_sum).astype(jnp.bfloat16)
    passed_on = shifted(block_cot, "section", -1)
    entering_full = entering_adjoint.astype(jnp.float32)
    fresh_rows = jnp.stack([(1.0 + GUIDE) * entering_full, -GUIDE * entering_full]).astype(
        jnp.bfloat16
    )
    is_last = lax.axis_index("section") == lax.axis_size("section") - 1
    return jnp.where(is_last, fresh_rows, passed_on)[None]


def solution(mesh):
    return jax.shard_map(
        shards,
        mesh=mesh,
        in_specs=(
            P("section", None, "tok", "head"),
            P("tok", "head"),
            P("section", "tok", "head"),
            P("section", "tok", "head"),
            P("section", None, "head"),
            P("section", "tok", "head"),
            P("section", None),
            P(),
            P(),
        ),
        out_specs=P("section", None, "tok", "head"),
        check_vma=False,
    )
```

profile of v0, /device:TPU:6, one launch (start us, length us, event | category | flops | bytes accessed | tf_op | source)
XLA Modules:
  0.0 357.0 jit_solution(16926532515218221262)
XLA Ops:
  6.5 0.0 copy-start
  6.5 0.0 all-gather.11.cloned.1.call-start
  6.5 1.9 copy.21
  8.4 0.0 all-gather.11.cloned.1.call-update
  8.4 0.0 all-gather.7.cloned.1.call-start
  8.5 0.7 all-gather.7.cloned.1.call-update
  9.2 0.0 all-gather.9.cloned.1.call-start
  9.2 0.7 all-gather.9.cloned.1.call-update
  9.9 0.0 reduce-scatter.5.cloned.1.call-start
  10.6 1.1 copy.20
  11.7 0.7 reduce
  12.4 1.1 select_reduce_fusion
  13.5 83.0 %all-gather.11.cloned.1.call-done = bf16[1,2048,640]{1,2,0:T(8,128)(2,1)} async-done(((bf16[1,128,640]{1,2,0:T(8,128)(2,1)}), bf16[1,2048,640]{1,2,0:T(8,128)(2,1)}) %all-gather.11.cloned.1.call-update) | async-done | bytes 2621456 | tf_op jit(solution)/shard_map/all_gather | solution.py:43
  96.6 2.7 multiply_reduce_fusion
  99.3 0.0 copy-start.1
  99.3 2.3 copy-done.1
  101.6 1.0 exponential_reduce_fusion
  102.6 21.9 %all-gather.7.cloned.1.call-done = bf16[1,2,128,2560]{3,2,1,0:T(8,128)(2,1)} async-done(((bf16[1,2,128,640]{3,2,1,0:T(8,128)(2,1)}), bf16[1,2,128,2560]{3,2,1,0:T(8,128)(2,1)}) %all-gather.7.cloned.1.call-update) | async-done | bytes 1310736 | tf_op jit(solution)/shard_map/all_gather | solution.py:33
  124.5 79.6 %all-gather.9.cloned.1.call-done = bf16[1,2560,640]{2,1,0:T(8,128)(2,1)} async-done(((bf16[1,160,640]{2,1,0:T(8,128)(2,1)}), bf16[1,2560,640]{2,1,0:T(8,128)(2,1)}) %all-gather.9.cloned.1.call-update) | async-done | bytes 3276816 | tf_op jit(solution)/shard_map/all_gather | solution.py:35
  204.2 3.5 fusion.9
  207.7 0.7 fusion.25
  208.4 0.8 copy.19
  209.2 5.3 %convolution_convert_fusion.1 = bf16[5,128,2048]{2,1,0:T(8,128)(2,1)} fusion(bf16[128,5,128]{0,2,1:T(8,128)(2,1)} %bitcast.51, f32[5,128,2048]{2,1,0:T(8,128)} %copy-done.1, f32[5,128]{1,0:T(8,128)S(1)} %log_add_fusion), kind=kOutput, calls=%fused_computation.7 | convolution fusion | flops 340787200 | bytes 8030720 | tf_op jit(solution)/shard_map/hij,ihe->jhe/dot_general | solution.py:54
  214.5 0.0 copy-start.2
  214.5 4.4 %copy.24 = bf16[2048,640]{1,0:T(8,128)(2,1)} copy(bf16[2048,640]{0,1:T(8,128)(2,1)} %bitcast.45) | data formatting | bytes 5242880 | tf_op jit(solution)/shard_map/convert_element_type | solution.py:56
  218.9 0.0 reduce-scatter.5.cloned.1.call-update
  218.9 0.0 reduce-scatter.7.cloned.1.call-start
  219.0 71.2 %reduce-scatter.5.cloned.1.call-done = bf16[128,640]{1,0:T(8,128)(2,1)} async-done(((bf16[2048,640]{1,0:T(8,128)(2,1)}), bf16[128,640]{1,0:T(8,128)(2,1)}) %reduce-scatter.5.cloned.1.call-update) | async-done | bytes 163856 | tf_op jit(solution)/shard_map/reduce_scatter | solution.py:55
  290.2 0.0 copy-done
  290.2 0.0 copy-done.2
  290.2 3.2 convolution_convert_fusion
  293.4 4.3 %copy.27 = bf16[2,128,2560]{1,0,2:T(2,128)(2,1)} copy(bf16[2,128,2560]{2,1,0:T(8,128)(2,1)} %convolution_convert_fusion) | data formatting | bytes 2621440
  297.7 0.0 copy-start.3
  297.7 2.6 copy.31
  300.3 0.0 reduce-scatter.7.cloned.1.call-update
  300.3 27.3 %reduce-scatter.7.cloned.1.call-done = bf16[640,256]{1,0:T(8,128)(2,1)} async-done(((bf16[2560,256]{1,0:T(8,128)(2,1)}), bf16[640,256]{1,0:T(8,128)(2,1)}) %reduce-scatter.7.cloned.1.call-update) | async-done | bytes 327696
  327.6 1.8 reshape.35
  329.4 1.9 copy.28
  331.3 1.9 fusion.14
  333.2 2.7 collective-permute-start
  336.0 0.0 copy-done.3
  336.0 12.7 %collective-permute-done = bf16[2,128,640]{2,1,0:T(8,128)(2,1)} collective-permute-done((bf16[2,128,640]{2,1,0:T(8,128)(2,1)}, bf16[2,128,640]{2,1,0:T(8,128)(2,1)}, u32[]{:S(2)}, u32[]{:S(2)}) %collective-permute-start) | collective-permute-done | bytes 327712 | tf_op jit(solution)/shard_map/ppermute | solution.py:13
  348.8 1.7 fusion.17
  (4 shorter events, 0.1 us)
Async XLA Ops:
  6.5 283.7 %copy-start = (bf16[1,2560,640]{2,1,0:T(8,128)(2,1)S(1)}, bf16[1,2560,640]{2,1,0:T(8,128)(2,1)}, u32[]{:S(2)}) copy-start(bf16[1,2560,640]{2,1,0:T(8,128)(2,1)} %param.13) | copy-start | bytes 9830404
  6.5 90.0 %all-gather.11.cloned.1.call-start = ((), (), s32[]{:S(2)}) async-start(), calls=%async_computation.5 | async-start | bytes 2785280 | tf_op jit(solution)/shard_map/all_gather | solution.py:43
  8.4 116.1 %all-gather.7.cloned.1.call-start = ((), (), s32[]{:S(2)}) async-start(), calls=%async_computation.3 | async-start | bytes 1638400 | tf_op jit(solution)/shard_map/all_gather | solution.py:33
  9.2 195.0 %all-gather.9.cloned.1.call-start = ((), (), s32[]{:S(2)}) async-start(), calls=%async_computation.4 | async-start | bytes 3481600 | tf_op jit(solution)/shard_map/all_gather | solution.py:35
  9.9 280.3 %reduce-scatter.5.cloned.1.call-start = ((), (), s32[]{:S(2)}) async-start(), calls=%async_computation.2 | async-start | bytes 2785280 | tf_op jit(solution)/shard_map/reduce_scatter | solution.py:55
  99.3 2.3 copy-start.1
  214.5 75.7 %copy-start.2 = (bf16[1,128,640]{2,1,0:T(8,128)(2,1)S(1)}, bf16[1,128,640]{2,1,0:T(8,128)(2,1)}, u32[]{:S(2)}) copy-start(bf16[1,128,640]{2,1,0:T(8,128)(2,1)} %get-tuple-element.6) | copy-start | bytes 491524
  218.9 108.7 %reduce-scatter.7.cloned.1.call-start = ((), (), s32[]{:S(2)}) async-start(), calls=%async_computation.6 | async-start | bytes 1638400
  297.7 38.3 %copy-start.3 = (bf16[128,640]{1,0:T(8,128)(2,1)S(1)}, bf16[128,640]{1,0:T(8,128)(2,1)}, u32[]{:S(2)}) copy-start(bf16[128,640]{1,0:T(8,128)(2,1)} %param.10) | copy-start | bytes 491524
  333.2 15.6 %collective-permute-start = (bf16[2,128,640]{2,1,0:T(8,128)(2,1)}, bf16[2,128,640]{2,1,0:T(8,128)(2,1)}, u32[]{:S(2)}, u32[]{:S(2)}) collective-permute-start(bf16[2,128,640]{2,1,0:T(8,128)(2,1)} %fusion.14), channel_id=1, source_target_pairs={{64,0},{128,64},{192,128},{256,192},{320,256},{384,320},{448,384},... | collective-permute-start | bytes 983048 | tf_op jit(solution)/shard_map/ppermute | solution.py:13
Sparse Core Ops, SparseCore 0:
  9.4 87.1 all-gather.10
  98.7 25.7 all-gather.6
  126.6 77.5 all-gather.8
  219.1 71.0 reduce-scatter.4
  300.4 27.1 reduce-scatter.6
where the time goes:
time: 358 us; the launch traced here: 357 us
  waiting for transfers between devices  297 us (83%)
  local copies, waits for them, and re-layouts  21.7 us (6%)
  matrix products  14.7 us (4%)
  between operations  13.9 us (4%)
  other arithmetic  6.49 us (2%)
    all_gather x1, waiting for transfers between devices, shards(): key_all = lax.all_gather(saved_keys[0], 'tok', axis=0, tiled=True)  83 us
    all_gather x1, waiting for transfers between devices, shards(): out_full = lax.all_gather(out_weight[0], 'tok', axis=0, tiled=True)  79.6 us
    reduce_scatter x1, waiting for transfers between devices, shards(): lax.psum_scatter(terms.reshape(lax.axis_size('tok') * rows_here, groups_h...  71.2 us
    unnamed x6, waiting for transfers between devices  28.7 us
    all_gather x1, waiting for transfers between devices, shards(): whole_cot = lax.all_gather(held_cotangents[0], 'head', axis=2, tiled=True)  21.9 us
    unnamed x14, local copies, waits for them, and re-layouts  15.8 us
    ppermute x1, waiting for transfers between devices, shifted(): lax.ppermute(value, axis, [(source, source + steps) for source in range(l...  12.7 us
  transfers between devices with their start and end apart: 6, of which 6 were waited for; matrix products, arithmetic and copies ran while one was open for 2% of the time, Pallas kernels for 0%

commit v1 on v0

--- a/solution.py
+++ b/solution.py
@@ -5,6 +5,22 @@
 
 HD = 128
 GUIDE = 3.0
+
+
+def product_in_turn(x, axis, dim, product):
+    size, index, rows = (lax.axis_size(axis), lax.axis_index(axis), x.shape[dim])
+    forward = [(i, (i + 1) % size) for i in range(size)]
+    left = [(i, (i - 1) % size) for i in range(size)]
+    middle = size // 2
+    from_left = from_right = x
+    so_far = product(x, index * rows)
+    for step in range(1, middle + 1):
+        from_left = lax.ppermute(from_left, axis, forward)
+        if step < size - middle:
+            from_right = lax.ppermute(from_right, axis, left)
+            so_far = so_far + product(from_right, (index + step) % size * rows)
+        so_far = so_far + product(from_left, (index - step) % size * rows)
+    return so_far
 
 
 def shifted(value, axis, steps):
@@ -32,9 +48,16 @@
     gate_row = block_gate[0] + time_row
     whole_cot = lax.all_gather(held_cotangents[0], "head", axis=2, tiled=True)
     scaled = (whole_cot.astype(jnp.float32) * gate_row).astype(jnp.bfloat16)
-    out_full = lax.all_gather(out_weight[0], "tok", axis=0, tiled=True)
-    attn_grad = jnp.einsum(
-        "btd,dk->btk", scaled, out_full, preferred_element_type=jnp.float32
+    attn_grad = product_in_turn(
+        out_weight[0],
+        "tok",
+        0,
+        lambda part, start: jnp.einsum(
+            "btd,dk->btk",
+            lax.dynamic_slice_in_dim(scaled, start, part.shape[0], axis=2),
+            part,
+            preferred_element_type=jnp.float32,
+        ),
     ).astype(jnp.bfloat16)
     rows_here = saved_queries.shape[1]
     groups_here = saved_queries.shape[2] // HD

time: 358 us -> 297 us (0.83)
  waiting for transfers between devices: 297 us -> 167 us
  starting transfers between devices: 2.91 us -> 61.4 us
  matrix products: 14.7 us -> 21.2 us
    all_gather x1 -> x0, waiting for transfers between devices: 79.6 us -> none  [shards(): out_full = lax.all_gather(out_weight[0], 'tok', axis=0, tiled=True)]
    ppermute x0 -> x15, starting transfers between devices: none -> 58.5 us  [the longest x7 41.3 us: product_in_turn(): from_right = lax.ppermute(from_right, axis, left)]
    all_gather x1, waiting for transfers between devices: 83 us -> 45 us  [shards(): key_all = lax.all_gather(saved_keys[0], 'tok', axis=0, tiled=True)]
    all_gather x1, waiting for transfers between devices: 21.9 us -> 0.02 us  [shards(): whole_cot = lax.all_gather(held_cotangents[0], 'head', axis=2, tiled=True)]
    ppermute x0 -> x15, waiting for transfers between devices: none -> 11 us  [the longest x8 9.84 us: product_in_turn(): from_left = lax.ppermute(from_left, axis, forward)]
    dot_general x1 -> x16, matrix products: 3.51 us -> 12.4 us  [shards(): jnp.einsum('btd,dk->btk', lax.dynamic_slice_in_dim(scaled, start, part.sh...]
    unnamed x14 -> x43, local copies, waits for them, and re-layouts: 15.8 us -> 17.7 us
    unnamed x6 -> x5, waiting for transfers between devices: 28.7 us -> 27.5 us
  transfers between devices with their start and end apart: 6 -> 20, of which waited for: 6 -> 12; matrix products, arithmetic and copies ran while one was open for 2% -> 7% of each run, Pallas kernels for 0% -> 0%
where the time goes in v1:
time: 297 us; the launch traced here: 295 us
  waiting for transfers between devices  167 us (56%)
  starting transfers between devices  61.4 us (21%)
  local copies, waits for them, and re-layouts  23.6 us (8%)
  matrix products  21.2 us (7%)
  between operations  14.6 us (5%)
  other arithmetic  7.54 us (3%)
    reduce_scatter x1, waiting for transfers between devices, shards(): lax.psum_scatter(terms.reshape(lax.axis_size('tok') * rows_here, groups_h...  70.8 us
    all_gather x1, waiting for transfers between devices, shards(): key_all = lax.all_gather(saved_keys[0], 'tok', axis=0, tiled=True)  45 us
    ppermute x7, starting transfers between devices, product_in_turn(): from_right = lax.ppermute(from_right, axis, left)  41.3 us
    unnamed x5, waiting for transfers between devices  27.5 us
    unnamed x43, local copies, waits for them, and re-layouts  17.7 us
    ppermute x8, starting transfers between devices, product_in_turn(): from_left = lax.ppermute(from_left, axis, forward)  17.2 us
    ppermute x1, waiting for transfers between devices, shifted(): lax.ppermute(value, axis, [(source, source + steps) for source in range(l...  12.7 us
    dot_general x16, matrix products, shards(): jnp.einsum('btd,dk->btk', lax.dynamic_slice_in_dim(scaled, start, part.sh...  12.4 us
  transfers between devices with their start and end apart: 20, of which 12 were waited for; matrix products, arithmetic and copies ran while one was open for 7% of the time, Pallas kernels for 0%

profile of v1, /device:TPU:6, one launch (start us, length us, event | category | flops | bytes accessed | tf_op | source)
XLA Modules:
  0.0 295.3 jit_solution(1169322400361874126)
XLA Ops:
  6.5 2.0 copy.21
  8.6 3.8 %collective-permute-start.1 = (bf16[160,640]{1,0:T(8,128)(2,1)}, bf16[160,640]{1,0:T(8,128)(2,1)S(1)}, u32[]{:S(2)}, u32[]{:S(2)}) collective-permute-start(bf16[160,640]{1,0:T(8,128)(2,1)} %bitcast.90), channel_id=1, source_target_pairs={{0,1},{1,2},{2,3},{3,4},{4,5},{5,6},{6,7},{7,8},{8,9},{9,10},{10,1... | collective-permute-start | bytes 614408 | tf_op jit(solution)/shard_map/ppermute | solution.py:18
  12.5 9.5 %collective-permute-start = (bf16[160,640]{1,0:T(8,128)(2,1)}, bf16[160,640]{1,0:T(8,128)(2,1)S(1)}, u32[]{:S(2)}, u32[]{:S(2)}) collective-permute-start(bf16[160,640]{1,0:T(8,128)(2,1)} %bitcast.91), channel_id=1, source_target_pairs={{0,15},{1,0},{2,1},{3,2},{4,3},{5,4},{6,5},{7,6},{8,7},{9,8},{10,9... | collective-permute-start | bytes 614408 | tf_op jit(solution)/shard_map/ppermute | solution.py:20
  22.0 3.3 %collective-permute-done.1 = bf16[160,640]{1,0:T(8,128)(2,1)S(1)} collective-permute-done((bf16[160,640]{1,0:T(8,128)(2,1)}, bf16[160,640]{1,0:T(8,128)(2,1)S(1)}, u32[]{:S(2)}, u32[]{:S(2)}) %collective-permute-start.1) | collective-permute-done | bytes 204832 | tf_op jit(solution)/shard_map/ppermute | solution.py:18
  25.3 1.9 collective-permute-start.3
  27.3 5.1 %collective-permute-start.2 = (bf16[160,640]{1,0:T(8,128)(2,1)S(1)}, bf16[160,640]{1,0:T(8,128)(2,1)S(1)}, u32[]{:S(2)}, u32[]{:S(2)}) collective-permute-start(bf16[160,640]{1,0:T(8,128)(2,1)S(1)} %collective-permute-done), channel_id=1, source_target_pairs={{0,15},{1,0},{2,1},{3,2},{4,3},{5,4},{6,5},{7,6},{8,7},{9,8},{10,9... | collective-permute-start | bytes 614408 | tf_op jit(solution)/shard_map/ppermute | solution.py:20
  32.4 2.3 collective-permute-done.3
  34.7 1.9 collective-permute-start.5
  36.6 5.1 %collective-permute-start.4 = (bf16[160,640]{1,0:T(8,128)(2,1)S(1)}, bf16[160,640]{1,0:T(8,128)(2,1)S(1)}, u32[]{:S(2)}, u32[]{:S(2)}) collective-permute-start(bf16[160,640]{1,0:T(8,128)(2,1)S(1)} %collective-permute-done.2), channel_id=1, source_target_pairs={{0,15},{1,0},{2,1},{3,2},{4,3},{5,4},{6,5},{7,6},{8,7},{9,8},{10,9... | collective-permute-start | bytes 614408 | tf_op jit(solution)/shard_map/ppermute | solution.py:20
  41.8 1.8 collective-permute-done.5
  43.5 1.9 collective-permute-start.7
  46.2 5.1 %collective-permute-start.6 = (bf16[160,640]{1,0:T(8,128)(2,1)S(1)}, bf16[160,640]{1,0:T(8,128)(2,1)}, u32[]{:S(2)}, u32[]{:S(2)}) collective-permute-start(bf16[160,640]{1,0:T(8,128)(2,1)S(1)} %collective-permute-done.4), channel_id=1, source_target_pairs={{0,15},{1,0},{2,1},{3,2},{4,3},{5,4},{6,5},{7,6},{8,7},{9,8},{10,9... | collective-permute-start | bytes 614408 | tf_op jit(solution)/shard_map/ppermute | solution.py:20
  51.3 1.1 collective-permute-done.7
  52.4 1.9 collective-permute-start.9
  54.6 5.7 %collective-permute-start.8 = (bf16[160,640]{1,0:T(8,128)(2,1)}, bf16[160,640]{1,0:T(8,128)(2,1)}, u32[]{:S(2)}, u32[]{:S(2)}) collective-permute-start(bf16[160,640]{1,0:T(8,128)(2,1)} %collective-permute-done.6), channel_id=1, source_target_pairs={{0,15},{1,0},{2,1},{3,2},{4,3},{5,4},{6,5},{7,6},{8,7},{9,8},{10,9... | collective-permute-start | bytes 614408 | tf_op jit(solution)/shard_map/ppermute | solution.py:20
  60.3 1.1 collective-permute-done.9
  61.4 1.9 collective-permute-start.11
  63.3 1.7 copy.24
  66.0 1.7 copy.23
  67.7 5.1 %collective-permute-start.10 = (bf16[160,640]{1,0:T(8,128)(2,1)}, bf16[160,640]{1,0:T(8,128)(2,1)}, u32[]{:S(2)}, u32[]{:S(2)}) collective-permute-start(bf16[160,640]{1,0:T(8,128)(2,1)} %collective-permute-done.8), channel_id=1, source_target_pairs={{0,15},{1,0},{2,1},{3,2},{4,3},{5,4},{6,5},{7,6},{8,7},{9,8},{10,9... | collective-permute-start | bytes 614408 | tf_op jit(solution)/shard_map/ppermute | solution.py:20
  72.9 1.9 collective-permute-start.13
  74.8 1.1 select_reduce_fusion
  76.9 5.6 %collective-permute-start.12 = (bf16[160,640]{1,0:T(8,128)(2,1)}, bf16[160,640]{1,0:T(8,128)(2,1)}, u32[]{:S(2)}, u32[]{:S(2)}) collective-permute-start(bf16[160,640]{1,0:T(8,128)(2,1)} %collective-permute-done.10), channel_id=1, source_target_pairs={{0,15},{1,0},{2,1},{3,2},{4,3},{5,4},{6,5},{7,6},{8,7},{9,8},{10,9... | collective-permute-start | bytes 614408 | tf_op jit(solution)/shard_map/ppermute | solution.py:20
  82.8 1.9 collective-permute-start.14
  84.8 1.8 fusion.1
  86.9 1.3 fusion.22
  88.2 1.3 fusion.25
  92.6 1.2 fusion.7
  93.9 1.2 fusion.6
  95.1 1.2 fusion.5
  96.4 1.2 fusion.19
  97.6 1.2 fusion.4
  98.9 1.2 fusion.10
  101.6 45.0 %all-gather.7.cloned.1.call-done = bf16[1,2048,640]{1,2,0:T(8,128)(2,1)} async-done(((bf16[1,128,640]{1,2,0:T(8,128)(2,1)}), bf16[1,2048,640]{1,2,0:T(8,128)(2,1)}) %all-gather.7.cloned.1.call-update) | async-done | bytes 2621456 | tf_op jit(solution)/shard_map/all_gather | solution.py:66
  146.6 2.8 multiply_reduce_fusion
  150.4 2.7 convolution_convert_fusion.1
  153.2 4.4 %copy.27 = bf16[2048,640]{1,0:T(8,128)(2,1)} copy(bf16[2048,640]{0,1:T(8,128)(2,1)} %bitcast.83) | data formatting | bytes 5242880 | tf_op jit(solution)/shard_map/convert_element_type | solution.py:79
  157.6 70.8 %reduce-scatter.5.cloned.1.call-done = bf16[128,640]{1,0:T(8,128)(2,1)} async-done(((bf16[2048,640]{1,0:T(8,128)(2,1)}), bf16[128,640]{1,0:T(8,128)(2,1)}) %reduce-scatter.5.cloned.1.call-update) | async-done | bytes 163856 | tf_op jit(solution)/shard_map/reduce_scatter | solution.py:78
  228.4 3.2 %convolution_convert_fusion = bf16[2,128,2560]{2,1,0:T(8,128)(2,1)} fusion(bf16[1,2560,640]{2,1,0:T(8,128)(2,1)S(1)} %copy-done, bf16[1,128,640]{2,1,0:T(8,128)(2,1)S(1)} %copy-done.15, bf16[1,128,640]{2,1,0:T(8,128)(2,1)} %bitcast.92), kind=kOutput, calls=%fused_computation.3 | convolution fusion | flops 839680000 | bytes 4915200 | tf_op jit(solution)/shard_map/btk,dk->btd/dot_general | solution.py:85
  231.6 4.3 %copy.30 = bf16[2,128,2560]{1,0,2:T(2,128)(2,1)} copy(bf16[2,128,2560]{2,1,0:T(8,128)(2,1)} %convolution_convert_fusion) | data formatting | bytes 2621440
  235.9 2.6 copy.34
  238.5 27.4 %reduce-scatter.7.cloned.1.call-done = bf16[640,256]{1,0:T(8,128)(2,1)} async-done(((bf16[2560,256]{1,0:T(8,128)(2,1)}), bf16[640,256]{1,0:T(8,128)(2,1)}) %reduce-scatter.7.cloned.1.call-update) | async-done | bytes 327696
  265.9 1.8 reshape.49
  267.7 1.9 copy.31
  269.6 1.9 fusion.11
  271.5 2.8 collective-permute-start.15
  274.4 12.7 %collective-permute-done.15 = bf16[2,128,640]{2,1,0:T(8,128)(2,1)} collective-permute-done((bf16[2,128,640]{2,1,0:T(8,128)(2,1)}, bf16[2,128,640]{2,1,0:T(8,128)(2,1)}, u32[]{:S(2)}, u32[]{:S(2)}) %collective-permute-start.15) | collective-permute-done | bytes 327712 | tf_op jit(solution)/shard_map/ppermute | solution.py:29
  287.1 1.7 fusion.14
  (71 shorter events, 8.4 us)
Async XLA Ops:
  6.5 221.9 %copy-start = (bf16[1,2560,640]{2,1,0:T(8,128)(2,1)S(1)}, bf16[1,2560,640]{2,1,0:T(8,128)(2,1)}, u32[]{:S(2)}) copy-start(bf16[1,2560,640]{2,1,0:T(8,128)(2,1)} %param.13) | copy-start | bytes 9830404
  6.5 61.2 %copy-start.17 = (f32[1,2560]{1,0:T(1,128)S(1)}, f32[1,2560]{1,0:T(1,128)}, u32[]{:S(2)}) copy-start(f32[1,2560]{1,0:T(1,128)} %param.15) | copy-start | bytes 30724
  6.5 78.2 %all-gather.5.cloned.1.call-start = ((), (), s32[]{:S(2)}) async-start(), calls=%async_computation.3 | async-start | bytes 1638400 | tf_op jit(solution)/shard_map/all_gather | solution.py:49
  8.6 138.0 %all-gather.7.cloned.1.call-start = ((), (), s32[]{:S(2)}) async-start(), calls=%async_computation.4 | async-start | bytes 2785280 | tf_op jit(solution)/shard_map/all_gather | solution.py:66
  8.6 16.7 %collective-permute-start.1 = (bf16[160,640]{1,0:T(8,128)(2,1)}, bf16[160,640]{1,0:T(8,128)(2,1)S(1)}, u32[]{:S(2)}, u32[]{:S(2)}) collective-permute-start(bf16[160,640]{1,0:T(8,128)(2,1)} %bitcast.90), channel_id=1, source_target_pairs={{0,1},{1,2},{2,3},{3,4},{4,5},{5,6},{6,7},{7,8},{8,9},{9,10},{10,1... | collective-permute-start | bytes 614408 | tf_op jit(solution)/shard_map/ppermute | solution.py:18
  12.5 14.8 %collective-permute-start = (bf16[160,640]{1,0:T(8,128)(2,1)}, bf16[160,640]{1,0:T(8,128)(2,1)S(1)}, u32[]{:S(2)}, u32[]{:S(2)}) collective-permute-start(bf16[160,640]{1,0:T(8,128)(2,1)} %bitcast.91), channel_id=1, source_target_pairs={{0,15},{1,0},{2,1},{3,2},{4,3},{5,4},{6,5},{7,6},{8,7},{9,8},{10,9... | collective-permute-start | bytes 614408 | tf_op jit(solution)/shard_map/ppermute | solution.py:20
  25.3 11.3 %copy-start.11 = (bf16[160,640]{1,0:T(8,128)(2,1)}, bf16[160,640]{1,0:T(8,128)(2,1)S(1)}, u32[]{:S(2)}) copy-start(bf16[160,640]{1,0:T(8,128)(2,1)S(1)} %collective-permute-done.1) | copy-start | bytes 614404
  25.3 9.4 %collective-permute-start.3 = (bf16[160,640]{1,0:T(8,128)(2,1)S(1)}, bf16[160,640]{1,0:T(8,128)(2,1)S(1)}, u32[]{:S(2)}, u32[]{:S(2)}) collective-permute-start(bf16[160,640]{1,0:T(8,128)(2,1)S(1)} %collective-permute-done.1), channel_id=1, source_target_pairs={{0,1},{1,2},{2,3},{3,4},{4,5},{5,6},{6,7},{7,8},{8,9},{9,10},{10,1... | collective-permute-start | bytes 614408 | tf_op jit(solution)/shard_map/ppermute | solution.py:18
  27.3 14.5 %copy-start.13 = (bf16[160,640]{1,0:T(8,128)(2,1)}, bf16[160,640]{1,0:T(8,128)(2,1)S(1)}, u32[]{:S(2)}) copy-start(bf16[160,640]{1,0:T(8,128)(2,1)S(1)} %collective-permute-done) | copy-start | bytes 614404
  27.3 9.4 %collective-permute-start.2 = (bf16[160,640]{1,0:T(8,128)(2,1)S(1)}, bf16[160,640]{1,0:T(8,128)(2,1)S(1)}, u32[]{:S(2)}, u32[]{:S(2)}) collective-permute-start(bf16[160,640]{1,0:T(8,128)(2,1)S(1)} %collective-permute-done), channel_id=1, source_target_pairs={{0,15},{1,0},{2,1},{3,2},{4,3},{5,4},{6,5},{7,6},{8,7},{9,8},{10,9... | collective-permute-start | bytes 614408 | tf_op jit(solution)/shard_map/ppermute | solution.py:20
  34.7 19.9 %copy-start.5 = (bf16[160,640]{1,0:T(8,128)(2,1)}, bf16[160,640]{1,0:T(8,128)(2,1)S(1)}, u32[]{:S(2)}) copy-start(bf16[160,640]{1,0:T(8,128)(2,1)S(1)} %collective-permute-done.3) | copy-start | bytes 614404
  34.7 8.9 %collective-permute-start.5 = (bf16[160,640]{1,0:T(8,128)(2,1)S(1)}, bf16[160,640]{1,0:T(8,128)(2,1)S(1)}, u32[]{:S(2)}, u32[]{:S(2)}) collective-permute-start(bf16[160,640]{1,0:T(8,128)(2,1)S(1)} %collective-permute-done.3), channel_id=1, source_target_pairs={{0,1},{1,2},{2,3},{3,4},{4,5},{5,6},{6,7},{7,8},{8,9},{9,10},{10,1... | collective-permute-start | bytes 614408 | tf_op jit(solution)/shard_map/ppermute | solution.py:18
  36.6 8.8 %collective-permute-start.4 = (bf16[160,640]{1,0:T(8,128)(2,1)S(1)}, bf16[160,640]{1,0:T(8,128)(2,1)S(1)}, u32[]{:S(2)}, u32[]{:S(2)}) collective-permute-start(bf16[160,640]{1,0:T(8,128)(2,1)S(1)} %collective-permute-done.2), channel_id=1, source_target_pairs={{0,15},{1,0},{2,1},{3,2},{4,3},{5,4},{6,5},{7,6},{8,7},{9,8},{10,9... | collective-permute-start | bytes 614408 | tf_op jit(solution)/shard_map/ppermute | solution.py:20
  43.5 16.7 %copy-start.7 = (bf16[160,640]{1,0:T(8,128)(2,1)}, bf16[160,640]{1,0:T(8,128)(2,1)S(1)}, u32[]{:S(2)}) copy-start(bf16[160,640]{1,0:T(8,128)(2,1)S(1)} %collective-permute-done.5) | copy-start | bytes 614404
  43.5 8.9 %collective-permute-start.7 = (bf16[160,640]{1,0:T(8,128)(2,1)S(1)}, bf16[160,640]{1,0:T(8,128)(2,1)S(1)}, u32[]{:S(2)}, u32[]{:S(2)}) collective-permute-start(bf16[160,640]{1,0:T(8,128)(2,1)S(1)} %collective-permute-done.5), channel_id=1, source_target_pairs={{0,1},{1,2},{2,3},{3,4},{4,5},{5,6},{6,7},{7,8},{8,9},{9,10},{10,1... | collective-permute-start | bytes 614408 | tf_op jit(solution)/shard_map/ppermute | solution.py:18
  45.5 0.7 copy-start.2
  46.2 8.4 %collective-permute-start.6 = (bf16[160,640]{1,0:T(8,128)(2,1)S(1)}, bf16[160,640]{1,0:T(8,128)(2,1)}, u32[]{:S(2)}, u32[]{:S(2)}) collective-permute-start(bf16[160,640]{1,0:T(8,128)(2,1)S(1)} %collective-permute-done.4), channel_id=1, source_target_pairs={{0,15},{1,0},{2,1},{3,2},{4,3},{5,4},{6,5},{7,6},{8,7},{9,8},{10,9... | collective-permute-start | bytes 614408 | tf_op jit(solution)/shard_map/ppermute | solution.py:20
  52.4 9.0 %copy-start.9 = (bf16[160,640]{1,0:T(8,128)(2,1)}, bf16[160,640]{1,0:T(8,128)(2,1)S(1)}, u32[]{:S(2)}) copy-start(bf16[160,640]{1,0:T(8,128)(2,1)S(1)} %collective-permute-done.7) | copy-start | bytes 614404
  52.4 9.0 %collective-permute-start.9 = (bf16[160,640]{1,0:T(8,128)(2,1)S(1)}, bf16[160,640]{1,0:T(8,128)(2,1)}, u32[]{:S(2)}, u32[]{:S(2)}) collective-permute-start(bf16[160,640]{1,0:T(8,128)(2,1)S(1)} %collective-permute-done.7), channel_id=1, source_target_pairs={{0,1},{1,2},{2,3},{3,4},{4,5},{5,6},{6,7},{7,8},{8,9},{9,10},{10,1... | collective-permute-start | bytes 614408 | tf_op jit(solution)/shard_map/ppermute | solution.py:18
  54.6 13.1 %collective-permute-start.8 = (bf16[160,640]{1,0:T(8,128)(2,1)}, bf16[160,640]{1,0:T(8,128)(2,1)}, u32[]{:S(2)}, u32[]{:S(2)}) collective-permute-start(bf16[160,640]{1,0:T(8,128)(2,1)} %collective-permute-done.6), channel_id=1, source_target_pairs={{0,15},{1,0},{2,1},{3,2},{4,3},{5,4},{6,5},{7,6},{8,7},{9,8},{10,9... | collective-permute-start | bytes 614408 | tf_op jit(solution)/shard_map/ppermute | solution.py:20
  61.4 11.5 %collective-permute-start.11 = (bf16[160,640]{1,0:T(8,128)(2,1)}, bf16[160,640]{1,0:T(8,128)(2,1)}, u32[]{:S(2)}, u32[]{:S(2)}) collective-permute-start(bf16[160,640]{1,0:T(8,128)(2,1)} %collective-permute-done.9), channel_id=1, source_target_pairs={{0,1},{1,2},{2,3},{3,4},{4,5},{5,6},{6,7},{7,8},{8,9},{9,10},{10,1... | collective-permute-start | bytes 614408 | tf_op jit(solution)/shard_map/ppermute | solution.py:18
  65.0 163.4 %reduce-scatter.5.cloned.1.call-start = ((), (), s32[]{:S(2)}) async-start(), calls=%async_computation.2 | async-start | bytes 2785280 | tf_op jit(solution)/shard_map/reduce_scatter | solution.py:78
  67.7 9.2 %collective-permute-start.10 = (bf16[160,640]{1,0:T(8,128)(2,1)}, bf16[160,640]{1,0:T(8,128)(2,1)}, u32[]{:S(2)}, u32[]{:S(2)}) collective-permute-start(bf16[160,640]{1,0:T(8,128)(2,1)} %collective-permute-done.8), channel_id=1, source_target_pairs={{0,15},{1,0},{2,1},{3,2},{4,3},{5,4},{6,5},{7,6},{8,7},{9,8},{10,9... | collective-permute-start | bytes 614408 | tf_op jit(solution)/shard_map/ppermute | solution.py:20
  72.9 9.9 %collective-permute-start.13 = (bf16[160,640]{1,0:T(8,128)(2,1)}, bf16[160,640]{1,0:T(8,128)(2,1)}, u32[]{:S(2)}, u32[]{:S(2)}) collective-permute-start(bf16[160,640]{1,0:T(8,128)(2,1)} %collective-permute-done.11), channel_id=1, source_target_pairs={{0,1},{1,2},{2,3},{3,4},{4,5},{5,6},{6,7},{7,8},{8,9},{9,10},{10,1... | collective-permute-start | bytes 614408 | tf_op jit(solution)/shard_map/ppermute | solution.py:18
  76.9 20.7 %collective-permute-start.12 = (bf16[160,640]{1,0:T(8,128)(2,1)}, bf16[160,640]{1,0:T(8,128)(2,1)}, u32[]{:S(2)}, u32[]{:S(2)}) collective-permute-start(bf16[160,640]{1,0:T(8,128)(2,1)} %collective-permute-done.10), channel_id=1, source_target_pairs={{0,15},{1,0},{2,1},{3,2},{4,3},{5,4},{6,5},{7,6},{8,7},{9,8},{10,9... | collective-permute-start | bytes 614408 | tf_op jit(solution)/shard_map/ppermute | solution.py:20
  82.8 16.1 %collective-permute-start.14 = (bf16[160,640]{1,0:T(8,128)(2,1)}, bf16[160,640]{1,0:T(8,128)(2,1)}, u32[]{:S(2)}, u32[]{:S(2)}) collective-permute-start(bf16[160,640]{1,0:T(8,128)(2,1)} %collective-permute-done.13), channel_id=1, source_target_pairs={{0,1},{1,2},{2,3},{3,4},{4,5},{5,6},{6,7},{7,8},{8,9},{9,10},{10,1... | collective-permute-start | bytes 614408 | tf_op jit(solution)/shard_map/ppermute | solution.py:18
  84.7 1.8 copy-start.4
  86.5 2.9 copy-start.10
  86.9 2.9 copy-start.8
  88.1 1.9 copy-start.6
  89.4 1.0 copy-start.14
  90.1 1.0 copy-start.12
  91.4 0.9 copy-start.3
  149.4 1.0 copy-start.1
  157.6 70.8 %copy-start.15 = (bf16[1,128,640]{2,1,0:T(8,128)(2,1)S(1)}, bf16[1,128,640]{2,1,0:T(8,128)(2,1)}, u32[]{:S(2)}) copy-start(bf16[1,128,640]{2,1,0:T(8,128)(2,1)} %get-tuple-element.6) | copy-start | bytes 491524
  157.6 108.4 %reduce-scatter.7.cloned.1.call-start = ((), (), s32[]{:S(2)}) async-start(), calls=%async_computation.5 | async-start | bytes 1638400
  238.5 35.8 %copy-start.16 = (bf16[128,640]{1,0:T(8,128)(2,1)S(1)}, bf16[128,640]{1,0:T(8,128)(2,1)}, u32[]{:S(2)}) copy-start(bf16[128,640]{1,0:T(8,128)(2,1)} %param.10) | copy-start | bytes 491524
  271.5 15.6 %collective-permute-start.15 = (bf16[2,128,640]{2,1,0:T(8,128)(2,1)}, bf16[2,128,640]{2,1,0:T(8,128)(2,1)}, u32[]{:S(2)}, u32[]{:S(2)}) collective-permute-start(bf16[2,128,640]{2,1,0:T(8,128)(2,1)} %fusion.11), channel_id=1, source_target_pairs={{64,0},{128,64},{192,128},{256,192},{320,256},{384,320},{448,384},... | collective-permute-start | bytes 983048 | tf_op jit(solution)/shard_map/ppermute | solution.py:29
Sparse Core Ops, SparseCore 0:
  9.5 34.6 all-gather.4
  65.1 81.4 all-gather.6
  157.7 70.6 reduce-scatter.4
  238.6 27.2 reduce-scatter.6
